TPU v7x, 512 devices: a whole 4x4x16 slice. The times are simulated.
512 devices in a mesh: leaf: 32 (over z, core), front: 16 (over x, y).
Axes of the slice: x: 4, y: 4, z: 16, core: 2. Of those that a mesh axis runs over, the one named last changes fastest.
Arguments:
- subtree_rhs: bfloat16 [524288, 256], P(('leaf', 'front')), may hold values from -6 to 6
- subtree_inverse: bfloat16 [524288, 1024], P(('leaf', 'front')), as said below
- coupling: bfloat16 [16384, 1024], P(('leaf', 'front')), may hold values from -0.1875 to 0.1875
- rhs_top: bfloat16 [4096, 256], P(('leaf', 'front')), may hold values from -6 to 6
- rhs_mid: bfloat16 [8192, 256], P(('leaf', 'front')), may hold values from -6 to 6
- rhs_low: bfloat16 [16384, 256], P(('leaf', 'front')), may hold values from -6 to 6
- inverse_top: bfloat16 [32, 16, 8, 4096], P(None, 'front', None, 'leaf'), as said below
- inverse_mid: bfloat16 [16, 16, 16, 8192], P(None, 'front', None, 'leaf'), as said below
- inverse_low: bfloat16 [8, 16, 32, 16384], P(None, 'front', None, 'leaf'), as said below
- update_mid: bfloat16 [16, 16, 16, 2, 4096], P(None, 'front', None, None, 'leaf'), may hold values from -0.0625 to 0.0625
- update_low: bfloat16 [8, 16, 32, 2, 8192], P(None, 'front', None, None, 'leaf'), may hold values from -0.0625 to 0.0625
- front_rows: int32 [7], replicated, may hold values from 1024 to 4096, as said below
Outputs:
- solution_sub: bfloat16 [524288, 256], P(('leaf', 'front'))
- solution_top: bfloat16 [4096, 256], P(('leaf', 'front'))
- solution_mid: bfloat16 [8192, 256], P(('leaf', 'front'))
- solution_low: bfloat16 [16384, 256], P(('leaf', 'front'))
Inputs may be any that keep to these rules, and one draw needn't show every extreme that they name: `front_rows`: live rows of the seven fronts in level order; each is a multiple of 128; the root has all 4096 rows, and at least one lowest front has all 4096 rows. `subtree_inverse`: each block of 1024 rows is a lower-triangular matrix with diagonal entries from 0.6 to 1.4. `inverse_top`: each front's block D is lower triangular with diagonal entries from 0.6 to 1.4. `inverse_mid`: each front's block D is lower triangular with diagonal entries from 0.6 to 1.4. `inverse_low`: each front's block D is lower triangular with diagonal entries from 0.6 to 1.4.
All inputs are finite; a program needn't handle non-finite values.
Results may differ from a plain program's by a relative error of at most 0.025.
Values may be sent and summed in bfloat16 or wider, within the bound.
No kernel may reach another device: no remote copies, remote signals or barrier semaphores. Data moves between devices by JAX's collectives and lax.ppermute only.
A program may use at most 64 MiB of HBM per device.

v0:
```python
import jax
import jax.numpy as jnp
from jax import lax
from jax.sharding import PartitionSpec as P


def partner(array, axis, distance):
    return lax.ppermute(array, axis, [(i, i ^ 1 << distance) for i in range(lax.axis_size(axis))])


def live_mask(front_rows, heap_start, groups, pieces):
    leaf_pos = lax.axis_index("leaf")
    front_pos = lax.axis_index("front")
    member = leaf_pos % groups
    node_pos = leaf_pos // groups
    lookup = jnp.arange(front_rows.shape[0], dtype=jnp.int32)
    live_rows = jnp.sum(jnp.where(lookup == heap_start + node_pos, front_rows, 0))
    front_ways = lax.axis_size("front")
    row_offset = (member * front_ways + front_pos) * pieces
    row_ids = row_offset + jnp.arange(pieces, dtype=jnp.int32)
    return (row_ids < live_rows)[:, None]


def group_gather(block, groups):
    leaf_pos = lax.axis_index("leaf")
    gathered = lax.all_gather(block, "leaf", axis=0, tiled=True)
    start_row = leaf_pos // groups * groups * block.shape[0]
    return lax.dynamic_slice_in_dim(gathered, start_row, groups * block.shape[0], 0)


def group_reduce(partial_value, groups):
    leaf_pos = lax.axis_index("leaf")
    current = partial_value.reshape(groups, -1, partial_value.shape[-1])
    for bit_pos in reversed(range(groups.bit_length() - 1)):
        half_count = current.shape[0] // 2
        lower_half = current[:half_count]
        upper_half = current[half_count:]
        upper_bit = leaf_pos // (1 << bit_pos) % 2
        kept_half = jnp.where(upper_bit == 0, lower_half, upper_half)
        sent_half = jnp.where(upper_bit == 0, upper_half, lower_half)
        current = kept_half + partner(sent_half.astype(jnp.bfloat16), "leaf", bit_pos).astype(
            sent_half.dtype
        )
    return current[0]


def forward_front(right_block, inverse, row_mask):
    groups = inverse.shape[0]
    pieces = inverse.shape[2]
    local_inverse = inverse.reshape(groups * pieces, inverse.shape[3])
    columns = group_gather(right_block, groups)
    summed = lax.psum_scatter(
        lax.dot_general(
            local_inverse, columns, (((0,), (0,)), ((), ())), preferred_element_type=jnp.float32
        ).astype(jnp.bfloat16),
        "front",
        scatter_dimension=0,
        tiled=True,
    ).astype(jnp.float32)
    return jnp.where(row_mask, summed, 0.0).astype(jnp.bfloat16)


def forward_update(child_solved, update, parent_rhs, parent_mask):
    groups = update.shape[0]
    pieces = update.shape[2]
    half_rows = update.shape[4]
    local_update = update.reshape(groups * pieces, 2 * half_rows)
    columns = group_gather(child_solved, groups)
    products = lax.dot_general(
        local_update, columns, (((0,), (0,)), ((), ())), preferred_element_type=jnp.float32
    )
    products = products.reshape(2, half_rows, columns.shape[1])
    parity = lax.axis_index("leaf") // groups % 2
    bit_pos = groups.bit_length() - 1
    kept_half = lax.dynamic_index_in_dim(products, parity, 0, keepdims=False)
    sent_half = lax.dynamic_index_in_dim(products, 1 - parity, 0, keepdims=False)
    both_sums = kept_half + partner(sent_half.astype(jnp.bfloat16), "leaf", bit_pos).astype(
        sent_half.dtype
    )
    summed = lax.psum_scatter(
        both_sums.astype(jnp.bfloat16), "front", scatter_dimension=0, tiled=True
    ).astype(jnp.float32)
    return jnp.where(parent_mask, parent_rhs.astype(jnp.float32) - summed, 0.0).astype(jnp.bfloat16)


def backward_front(solved_block, inverse, row_mask):
    groups = inverse.shape[0]
    pieces = inverse.shape[2]
    local_inverse = inverse.reshape(groups * pieces, inverse.shape[3])

    def add_rows(running, piece_rows, start_row):
        return jnp.dot(local_inverse, piece_rows, preferred_element_type=jnp.float32)

    initial = jnp.zeros((groups * pieces, solved_block.shape[1]), jnp.float32)
    partial_value = add_rows(
        initial, lax.all_gather(solved_block, "front", axis=0, tiled=True), jnp.int32(0)
    )
    summed = group_reduce(partial_value, groups)
    return jnp.where(row_mask, summed, 0.0).astype(jnp.bfloat16)


def backward_update(child_forward, update, parent_solution, row_mask):
    groups = update.shape[0]
    pieces = update.shape[2]
    half_rows = update.shape[4]
    local_update = update.reshape(groups * pieces, 2, half_rows)
    parity = lax.axis_index("leaf") // groups % 2
    bit_pos = groups.bit_length() - 1
    sibling_block = partner(parent_solution, "leaf", bit_pos)
    own_update = lax.dynamic_index_in_dim(local_update, parity, 1, keepdims=False)
    other_update = lax.dynamic_index_in_dim(local_update, 1 - parity, 1, keepdims=False)

    def add_rows(running, pieces_pair, start_row):
        own_rows, other_rows = pieces_pair
        running = jnp.dot(own_update, own_rows, preferred_element_type=jnp.float32)
        return running + jnp.dot(other_update, other_rows, preferred_element_type=jnp.float32)

    initial = jnp.zeros((groups * pieces, parent_solution.shape[1]), jnp.float32)
    partial_value = add_rows(
        initial,
        (
            lax.all_gather(parent_solution, "front", axis=0, tiled=True),
            lax.all_gather(sibling_block, "front", axis=0, tiled=True),
        ),
        jnp.int32(0),
    )
    summed = group_reduce(partial_value, groups)
    return jnp.where(row_mask, child_forward.astype(jnp.float32) - summed, 0.0).astype(jnp.bfloat16)


def shards(
    subtree_rhs,
    subtree_inverse,
    coupling,
    rhs_top,
    rhs_mid,
    rhs_low,
    inverse_top,
    inverse_mid,
    inverse_low,
    update_mid,
    update_low,
    front_rows,
):
    below_solved = jnp.dot(subtree_inverse, subtree_rhs, preferred_element_type=jnp.float32).astype(
        jnp.bfloat16
    )
    mask_top = live_mask(front_rows, 0, inverse_top.shape[0], rhs_top.shape[0])
    mask_mid = live_mask(front_rows, 1, inverse_mid.shape[0], rhs_mid.shape[0])
    mask_low = live_mask(front_rows, 3, inverse_low.shape[0], rhs_low.shape[0])
    pushed = jnp.dot(coupling, below_solved, preferred_element_type=jnp.float32)
    right_low = jnp.where(mask_low, rhs_low.astype(jnp.float32) - pushed, 0.0).astype(jnp.bfloat16)
    forward_low = forward_front(right_low, inverse_low, mask_low)
    right_mid = forward_update(forward_low, update_low, rhs_mid, mask_mid)
    forward_mid = forward_front(right_mid, inverse_mid, mask_mid)
    right_top = forward_update(forward_mid, update_mid, rhs_top, mask_top)
    forward_top = forward_front(right_top, inverse_top, mask_top)
    solution_top = backward_front(forward_top, inverse_top, mask_top)
    residual_mid = backward_update(forward_mid, update_mid, solution_top, mask_mid)
    solution_mid = backward_front(residual_mid, inverse_mid, mask_mid)
    residual_low = backward_update(forward_low, update_low, solution_mid, mask_low)
    solution_low = backward_front(residual_low, inverse_low, mask_low)
    moved = lax.dot_general(
        coupling, solution_low, (((0,), (0,)), ((), ())), preferred_element_type=jnp.float32
    )
    shifted = (below_solved.astype(jnp.float32) - moved).astype(jnp.bfloat16)
    solution_sub = lax.dot_general(
        subtree_inverse, shifted, (((0,), (0,)), ((), ())), preferred_element_type=jnp.float32
    ).astype(jnp.bfloat16)
    return (solution_sub, solution_top, solution_mid, solution_low)


def solution(mesh):
    placed = (
        P(("leaf", "front"), None),
        P(("leaf", "front"), None),
        P(("leaf", "front"), None),
        P(("leaf", "front"), None),
        P(("leaf", "front"), None),
        P(("leaf", "front"), None),
        P(None, "front", None, "leaf"),
        P(None, "front", None, "leaf"),
        P(None, "front", None, "leaf"),
        P(None, "front", None, None, "leaf"),
        P(None, "front", None, None, "leaf"),
        P(),
    )
    return jax.shard_map(
        shards,
        mesh=mesh,
        in_specs=placed,
        out_specs=(
            P(("leaf", "front"), None),
            P(("leaf", "front"), None),
            P(("leaf", "front"), None),
            P(("leaf", "front"), None),
        ),
        check_vma=False,
    )
```

profile of v0, /device:TPU:1, one launch (start us, length us, event | category | flops | bytes accessed | tf_op | source)
XLA Modules:
  0.0 1013.0 jit_solution(10693021480637807636)
XLA Ops:
  12.2 39.0 %all_gather.36 = bf16[1024,256]{1,0:T(8,128)(2,1)S(1)} all-gather(bf16[32,256]{1,0:T(8,128)(2,1)S(1)} %fusion.8), channel_id=1, replica_groups=mesh['leaf'=32,'front'=16] {'leaf'}, dimensions={0}, use_global_device_ids=true | all-gather | bytes 540672 | tf_op jit(solution)/shard_map/all_gather | solution.py:26
  52.4 81.3 %reduce-scatter.10.cloned.1.call-done = bf16[32,256]{1,0:T(8,128)(2,1)} async-done(((bf16[512,256]{1,0:T(8,128)(2,1)}), bf16[32,256]{1,0:T(8,128)(2,1)}) %reduce-scatter.10.cloned.1.call-update) | async-done | bytes 16400 | tf_op jit(solution)/shard_map/reduce_scatter | solution.py:52
  134.5 34.5 %all_gather.37 = bf16[1024,256]{1,0:T(8,128)(2,1)S(1)} all-gather(bf16[32,256]{1,0:T(8,128)(2,1)S(1)} %select_convert_fusion.15), channel_id=1, replica_groups=mesh['leaf'=32,'front'=16] {'leaf'}, dimensions={0}, use_global_device_ids=true | all-gather | bytes 540672 | tf_op jit(solution)/shard_map/all_gather | solution.py:26
  169.9 4.7 collective-permute-start
  174.9 14.5 %collective-permute-done = bf16[256,256]{0,1:T(8,128)(2,1)} collective-permute-done((bf16[256,256]{0,1:T(8,128)(2,1)S(1)}, bf16[256,256]{0,1:T(8,128)(2,1)}, u32[]{:S(2)}, u32[]{:S(2)}) %collective-permute-start) | collective-permute-done | bytes 131104 | tf_op jit(solution)/shard_map/ppermute | solution.py:8
  191.8 80.4 %reduce-scatter.12.cloned.1.call-done = bf16[16,256]{1,0:T(8,128)(2,1)} async-done(((bf16[256,256]{1,0:T(8,128)(2,1)}), bf16[16,256]{1,0:T(8,128)(2,1)}) %reduce-scatter.12.cloned.1.call-update) | async-done | bytes 8208 | tf_op jit(solution)/shard_map/reduce_scatter | solution.py:80
  273.0 34.1 %all_gather.38 = bf16[512,256]{1,0:T(8,128)(2,1)S(1)} all-gather(bf16[16,256]{1,0:T(8,128)(2,1)S(1)} %select_convert_fusion.20), channel_id=1, replica_groups=mesh['leaf'=32,'front'=16] {'leaf'}, dimensions={0}, use_global_device_ids=true | all-gather | bytes 270336 | tf_op jit(solution)/shard_map/all_gather | solution.py:26
  308.2 80.8 %reduce-scatter.14.cloned.1.call-done = bf16[16,256]{1,0:T(8,128)(2,1)} async-done(((bf16[256,256]{1,0:T(8,128)(2,1)}), bf16[16,256]{1,0:T(8,128)(2,1)}) %reduce-scatter.14.cloned.1.call-update) | async-done | bytes 8208 | tf_op jit(solution)/shard_map/reduce_scatter | solution.py:52
  389.8 34.1 %all_gather.39 = bf16[512,256]{1,0:T(8,128)(2,1)S(1)} all-gather(bf16[16,256]{1,0:T(8,128)(2,1)S(1)} %select_convert_fusion.19), channel_id=1, replica_groups=mesh['leaf'=32,'front'=16] {'leaf'}, dimensions={0}, use_global_device_ids=true | all-gather | bytes 270336 | tf_op jit(solution)/shard_map/all_gather | solution.py:26
  424.1 8.9 collective-permute-start.1
  435.0 3.2 collective-permute-done.1
  439.6 108.8 %all-reduce.5.cloned.1.call-done = bf16[128,256]{1,0:T(8,128)(2,1)} async-done(((bf16[128,256]{1,0:T(8,128)(2,1)}), bf16[128,256]{1,0:T(8,128)(2,1)}) %all-reduce.5.cloned.1.call-update) | async-done | bytes 65552
  549.2 33.4 %all_gather.40 = bf16[256,256]{1,0:T(8,128)(2,1)S(1)} all-gather(bf16[8,256]{1,0:T(8,128)(2,1)S(1)} %select_convert_fusion.23), channel_id=1, replica_groups=mesh['leaf'=32,'front'=16] {'leaf'}, dimensions={0}, use_global_device_ids=true | all-gather | bytes 135168 | tf_op jit(solution)/shard_map/all_gather | solution.py:26
  584.5 105.7 %all-reduce.7.cloned.1.call-done = bf16[128,256]{1,0:T(8,128)(2,1)} async-done(((bf16[128,256]{1,0:T(8,128)(2,1)}), bf16[128,256]{1,0:T(8,128)(2,1)}) %all-reduce.7.cloned.1.call-update) | async-done | bytes 65552
  690.9 17.5 %all_gather.41 = bf16[128,256]{1,0:T(8,128)(2,1)S(1)} all-gather(bf16[8,256]{1,0:T(8,128)(2,1)S(1)} %select_convert_fusion.22), channel_id=1, replica_groups=mesh['leaf'=32,'front'=16] {'front'}, dimensions={0}, use_global_device_ids=true | all-gather | bytes 69632 | tf_op jit(solution)/shard_map/all_gather | solution.py:96
  709.4 12.5 %collective-permute-start.2 = (bf16[16,8,256]{2,1,0:T(8,128)(2,1)S(1)}, bf16[16,8,256]{2,1,0:T(8,128)(2,1)S(1)}, u32[]{:S(2)}, u32[]{:S(2)}) collective-permute-start(bf16[16,8,256]{2,1,0:T(8,128)(2,1)S(1)} %fusion.26), channel_id=1, source_target_pairs={{0,256},{16,272},{32,288},{48,304},{64,320},{80,336},{96,352},{112... | collective-permute-start | bytes 196616 | tf_op jit(solution)/shard_map/ppermute | solution.py:8
  723.9 7.9 collective-permute-start.3
  731.9 3.9 collective-permute-done.3
  735.8 2.6 collective-permute-start.4
  738.4 2.8 collective-permute-done.4
  743.2 2.5 collective-permute-done.5
  745.7 12.3 %collective-permute-start.6 = (bf16[1,8,256]{2,1,0:T(8,128)(2,1)S(1)}, bf16[1,8,256]{2,1,0:T(8,128)(2,1)S(1)}, u32[]{:S(2)}, u32[]{:S(2)}) collective-permute-start(bf16[1,8,256]{2,1,0:T(8,128)(2,1)S(1)} %select_convert_fusion.21), channel_id=1, source_target_pairs={{0,16},{16,0},{32,48},{48,32},{64,80},{80,64},{96,112},{112,96},{1... | collective-permute-start | bytes 12296 | tf_op jit(solution)/shard_map/ppermute | solution.py:8
  758.8 15.9 %all_gather.42 = bf16[128,256]{1,0:T(8,128)(2,1)S(1)} all-gather(bf16[8,256]{1,0:T(8,128)(2,1)S(1)} %fusion.40), channel_id=1, replica_groups=mesh['leaf'=32,'front'=16] {'front'}, dimensions={0}, use_global_device_ids=true | all-gather | bytes 69632 | tf_op jit(solution)/shard_map/all_gather | solution.py:122
  774.7 13.4 %collective-permute-start.7 = (bf16[8,256]{1,0:T(8,128)(2,1)S(1)}, bf16[8,256]{1,0:T(8,128)(2,1)S(1)}, u32[]{:S(2)}, u32[]{:S(2)}) collective-permute-start(bf16[8,256]{1,0:T(8,128)(2,1)S(1)} %fusion.40), channel_id=1, source_target_pairs={{0,256},{16,272},{32,288},{48,304},{64,320},{80,336},{96,352},{112... | collective-permute-start | bytes 12296 | tf_op jit(solution)/shard_map/ppermute | solution.py:8
  789.1 17.8 %all_gather.43 = bf16[128,256]{1,0:T(8,128)(2,1)S(1)} all-gather(bf16[8,256]{1,0:T(8,128)(2,1)S(1)} %collective-permute-done.7), channel_id=1, replica_groups=mesh['leaf'=32,'front'=16] {'front'}, dimensions={0}, use_global_device_ids=true | all-gather | bytes 69632 | tf_op jit(solution)/shard_map/all_gather | solution.py:123
  807.1 5.3 collective-permute-start.8
  812.5 5.2 collective-permute-done.8
  819.6 3.6 collective-permute-done.9
  825.2 2.9 collective-permute-done.10
  828.0 16.8 %collective-permute-start.11 = (bf16[1,16,256]{2,1,0:T(8,128)(2,1)S(1)}, bf16[1,16,256]{2,1,0:T(8,128)(2,1)S(1)}, u32[]{:S(2)}, u32[]{:S(2)}) collective-permute-start(bf16[1,16,256]{2,1,0:T(8,128)(2,1)S(1)} %select_convert_fusion.17), channel_id=1, source_target_pairs={{0,16},{16,0},{32,48},{48,32},{64,80},{80,64},{96,112},{112,96},{1... | collective-permute-start | bytes 24584 | tf_op jit(solution)/shard_map/ppermute | solution.py:8
  845.7 16.0 %all_gather.44 = bf16[256,256]{1,0:T(8,128)(2,1)S(1)} all-gather(bf16[16,256]{1,0:T(8,128)(2,1)S(1)} %fusion.39), channel_id=1, replica_groups=mesh['leaf'=32,'front'=16] {'front'}, dimensions={0}, use_global_device_ids=true | all-gather | bytes 139264 | tf_op jit(solution)/shard_map/all_gather | solution.py:96
  862.0 4.4 collective-permute-start.12
  866.4 5.5 collective-permute-done.12
  873.9 5.0 collective-permute-done.13
  880.9 2.5 collective-permute-done.14
  883.4 10.0 collective-permute-start.15
  894.3 17.4 %all_gather.45 = bf16[256,256]{1,0:T(8,128)(2,1)S(1)} all-gather(bf16[16,256]{1,0:T(8,128)(2,1)S(1)} %fusion.37), channel_id=1, replica_groups=mesh['leaf'=32,'front'=16] {'front'}, dimensions={0}, use_global_device_ids=true | all-gather | bytes 139264 | tf_op jit(solution)/shard_map/all_gather | solution.py:122
  911.7 3.6 collective-permute-start.16
  915.5 4.5 collective-permute-done.16
  920.0 16.0 %all_gather.46 = bf16[256,256]{1,0:T(8,128)(2,1)S(1)} all-gather(bf16[16,256]{1,0:T(8,128)(2,1)S(1)} %collective-permute-done.16), channel_id=1, replica_groups=mesh['leaf'=32,'front'=16] {'front'}, dimensions={0}, use_global_device_ids=true | all-gather | bytes 139264 | tf_op jit(solution)/shard_map/all_gather | solution.py:123
  936.2 2.1 collective-permute-start.17
  938.3 4.2 collective-permute-done.17
  944.5 3.0 collective-permute-done.18
  947.5 16.4 %collective-permute-start.19 = (bf16[1,32,256]{2,1,0:T(8,128)(2,1)S(1)}, bf16[1,32,256]{2,1,0:T(8,128)(2,1)S(1)}, u32[]{:S(2)}, u32[]{:S(2)}) collective-permute-start(bf16[1,32,256]{2,1,0:T(8,128)(2,1)S(1)} %select_convert_fusion.11), channel_id=1, source_target_pairs={{0,16},{16,0},{32,48},{48,32},{64,80},{80,64},{96,112},{112,96},{1... | collective-permute-start | bytes 49160 | tf_op jit(solution)/shard_map/ppermute | solution.py:8
  964.8 17.5 %all_gather.47 = bf16[512,256]{1,0:T(8,128)(2,1)S(1)} all-gather(bf16[32,256]{1,0:T(8,128)(2,1)S(1)} %fusion.36), channel_id=1, replica_groups=mesh['leaf'=32,'front'=16] {'front'}, dimensions={0}, use_global_device_ids=true | all-gather | bytes 278528 | tf_op jit(solution)/shard_map/all_gather | solution.py:96
  984.5 4.1 collective-permute-done.20
  990.6 2.7 collective-permute-done.21
  993.4 10.1 collective-permute-start.22
  (145 shorter events, 46.3 us)
Async XLA Ops:
  7.2 1.6 copy-start
  7.2 126.5 %reduce-scatter.10.cloned.1.call-start = ((), (), s32[]{:S(2)}) async-start(), calls=%async_computation.3 | async-start | bytes 278528 | tf_op jit(solution)/shard_map/reduce_scatter | solution.py:52
  8.8 1.9 copy-start.18
  8.8 3.2 copy-start.9
  8.8 3.2 copy-start.13
  8.8 42.4 %copy-start.1 = (bf16[8,1,32,512]{3,2,1,0:T(8,128)(2,1)S(1)}, bf16[8,1,32,512]{3,2,1,0:T(8,128)(2,1)}, u32[]{:S(2)}) copy-start(bf16[8,1,32,512]{3,2,1,0:T(8,128)(2,1)} %param.20) | copy-start | bytes 786436
  10.6 1.4 copy-start.5
  10.6 41.8 %copy-start.2 = (bf16[8,1,32,2,256]{4,3,2,1,0:T(2,128)(2,1)S(1)}, bf16[8,1,32,2,256]{4,3,2,1,0:T(2,128)(2,1)}, u32[]{:S(2)}) copy-start(bf16[8,1,32,2,256]{4,3,2,1,0:T(2,128)(2,1)} %param.22) | copy-start | bytes 786436
  52.3 219.9 %reduce-scatter.12.cloned.1.call-start = ((), (), s32[]{:S(2)}) async-start(), calls=%async_computation.4 | async-start | bytes 139264 | tf_op jit(solution)/shard_map/reduce_scatter | solution.py:80
  169.0 103.2 %copy-start.16 = (bf16[16,256]{1,0:T(8,128)(2,1)S(1)}, bf16[16,256]{1,0:T(8,128)(2,1)}, u32[]{:S(2)}) copy-start(bf16[16,256]{1,0:T(8,128)(2,1)} %param.16) | copy-start | bytes 24580
  169.3 137.9 %copy-start.7 = (bf16[16,1,16,256]{3,2,1,0:T(8,128)(2,1)S(1)}, bf16[16,1,16,256]{3,2,1,0:T(8,128)(2,1)}, u32[]{:S(2)}) copy-start(bf16[16,1,16,256]{3,2,1,0:T(8,128)(2,1)} %param.19) | copy-start | bytes 393220
  169.6 254.2 %copy-start.4 = (bf16[16,1,16,2,128]{4,3,2,1,0:T(2,128)(2,1)S(1)}, bf16[16,1,16,2,128]{4,3,2,1,0:T(2,128)(2,1)}, u32[]{:S(2)}) copy-start(bf16[16,1,16,2,128]{4,3,2,1,0:T(2,128)(2,1)} %param.21) | copy-start | bytes 393220
  169.9 378.6 %copy-start.17 = (bf16[8,256]{1,0:T(8,128)(2,1)S(1)}, bf16[8,256]{1,0:T(8,128)(2,1)}, u32[]{:S(2)}) copy-start(bf16[8,256]{1,0:T(8,128)(2,1)} %param.15) | copy-start | bytes 12292
  169.9 19.4 %collective-permute-start = (bf16[256,256]{0,1:T(8,128)(2,1)S(1)}, bf16[256,256]{0,1:T(8,128)(2,1)}, u32[]{:S(2)}, u32[]{:S(2)}) collective-permute-start(bf16[256,256]{0,1:T(8,128)(2,1)S(1)} %bitcast.156), channel_id=1, source_target_pairs={{0,128},{16,144},{32,160},{48,176},{64,192},{80,208},{96,224},{112... | collective-permute-start | bytes 393224 | tf_op jit(solution)/shard_map/ppermute | solution.py:8
  191.1 197.9 %reduce-scatter.14.cloned.1.call-start = ((), (), s32[]{:S(2)}) async-start(), calls=%async_computation.5 | async-start | bytes 139264 | tf_op jit(solution)/shard_map/reduce_scatter | solution.py:52
  308.2 240.3 %all-reduce.5.cloned.1.call-start = ((), (), s32[]{:S(2)}) async-start(), calls=%async_computation.6 | async-start | bytes 131072
  424.1 14.1 %collective-permute-start.1 = (bf16[128,256]{1,0:T(8,128)(2,1)S(1)}, bf16[128,256]{1,0:T(8,128)(2,1)S(1)}, u32[]{:S(2)}, u32[]{:S(2)}) collective-permute-start(bf16[128,256]{1,0:T(8,128)(2,1)S(1)} %fusion.25), channel_id=1, source_target_pairs={{0,256},{16,272},{32,288},{48,304},{64,320},{80,336},{96,352},{112... | collective-permute-start | bytes 196616 | tf_op jit(solution)/shard_map/ppermute | solution.py:8
  438.9 251.2 %all-reduce.7.cloned.1.call-start = ((), (), s32[]{:S(2)}) async-start(), calls=%async_computation.7 | async-start | bytes 131072
  709.4 136.3 %copy-start.12 = (bf16[16,256]{1,0:T(8,128)(2,1)S(1)}, bf16[16,256]{1,0:T(8,128)(2,1)}, u32[]{:S(2)}) copy-start(bf16[16,256]{1,0:T(8,128)(2,1)} %reduce-scatter.14.cloned.1.call-done) | copy-start | bytes 24580
  709.4 14.5 %collective-permute-start.2 = (bf16[16,8,256]{2,1,0:T(8,128)(2,1)S(1)}, bf16[16,8,256]{2,1,0:T(8,128)(2,1)S(1)}, u32[]{:S(2)}, u32[]{:S(2)}) collective-permute-start(bf16[16,8,256]{2,1,0:T(8,128)(2,1)S(1)} %fusion.26), channel_id=1, source_target_pairs={{0,256},{16,272},{32,288},{48,304},{64,320},{80,336},{96,352},{112... | collective-permute-start | bytes 196616 | tf_op jit(solution)/shard_map/ppermute | solution.py:8
  723.9 11.9 %collective-permute-start.3 = (bf16[8,8,256]{2,1,0:T(8,128)(2,1)S(1)}, bf16[8,8,256]{2,1,0:T(8,128)(2,1)S(1)}, u32[]{:S(2)}, u32[]{:S(2)}) collective-permute-start(bf16[8,8,256]{2,1,0:T(8,128)(2,1)S(1)} %select_convert_fusion.9), channel_id=1, source_target_pairs={{0,128},{16,144},{32,160},{48,176},{64,192},{80,208},{96,224},{112... | collective-permute-start | bytes 98312 | tf_op jit(solution)/shard_map/ppermute | solution.py:8
  735.8 5.4 collective-permute-start.4
  741.2 4.4 collective-permute-start.5
  745.7 13.1 %collective-permute-start.6 = (bf16[1,8,256]{2,1,0:T(8,128)(2,1)S(1)}, bf16[1,8,256]{2,1,0:T(8,128)(2,1)S(1)}, u32[]{:S(2)}, u32[]{:S(2)}) collective-permute-start(bf16[1,8,256]{2,1,0:T(8,128)(2,1)S(1)} %select_convert_fusion.21), channel_id=1, source_target_pairs={{0,16},{16,0},{32,48},{48,32},{64,80},{80,64},{96,112},{112,96},{1... | collective-permute-start | bytes 12296 | tf_op jit(solution)/shard_map/ppermute | solution.py:8
  758.8 113.1 %copy-start.15 = (bf16[8,256]{1,0:T(8,128)(2,1)}, bf16[8,256]{1,0:T(8,128)(2,1)S(1)}, u32[]{:S(2)}) copy-start(bf16[8,256]{1,0:T(8,128)(2,1)S(1)} %fusion.40) | copy-start | bytes 12292
  774.7 14.4 %collective-permute-start.7 = (bf16[8,256]{1,0:T(8,128)(2,1)S(1)}, bf16[8,256]{1,0:T(8,128)(2,1)S(1)}, u32[]{:S(2)}, u32[]{:S(2)}) collective-permute-start(bf16[8,256]{1,0:T(8,128)(2,1)S(1)} %fusion.40), channel_id=1, source_target_pairs={{0,256},{16,272},{32,288},{48,304},{64,320},{80,336},{96,352},{112... | collective-permute-start | bytes 12296 | tf_op jit(solution)/shard_map/ppermute | solution.py:8
  806.9 86.5 %copy-start.3 = (bf16[8,1,32,2,256]{4,3,2,1,0:T(2,128)(2,1)S(1)}, bf16[8,1,32,2,256]{4,3,2,1,0:T(2,128)(2,1)}, u32[]{:S(2)}) copy-start(bf16[8,1,32,2,256]{4,3,2,1,0:T(2,128)(2,1)} %param.22) | copy-start | bytes 786436
  807.1 10.5 %collective-permute-start.8 = (bf16[8,16,256]{2,1,0:T(8,128)(2,1)S(1)}, bf16[8,16,256]{2,1,0:T(8,128)(2,1)S(1)}, u32[]{:S(2)}, u32[]{:S(2)}) collective-permute-start(bf16[8,16,256]{2,1,0:T(8,128)(2,1)S(1)} %bitcast.159), channel_id=1, source_target_pairs={{0,128},{16,144},{32,160},{48,176},{64,192},{80,208},{96,224},{112... | collective-permute-start | bytes 196616 | tf_op jit(solution)/shard_map/ppermute | solution.py:8
  817.6 5.6 collective-permute-start.9
  823.2 4.8 collective-permute-start.10
  828.0 17.6 %collective-permute-start.11 = (bf16[1,16,256]{2,1,0:T(8,128)(2,1)S(1)}, bf16[1,16,256]{2,1,0:T(8,128)(2,1)S(1)}, u32[]{:S(2)}, u32[]{:S(2)}) collective-permute-start(bf16[1,16,256]{2,1,0:T(8,128)(2,1)S(1)} %select_convert_fusion.17), channel_id=1, source_target_pairs={{0,16},{16,0},{32,48},{48,32},{64,80},{80,64},{96,112},{112,96},{1... | collective-permute-start | bytes 24584 | tf_op jit(solution)/shard_map/ppermute | solution.py:8
  862.0 10.0 collective-permute-start.12
  871.9 92.8 %copy-start.8 = (bf16[32,256]{1,0:T(8,128)(2,1)S(1)}, bf16[32,256]{1,0:T(8,128)(2,1)}, u32[]{:S(2)}) copy-start(bf16[32,256]{1,0:T(8,128)(2,1)} %reduce-scatter.10.cloned.1.call-done) | copy-start | bytes 49156
  872.0 6.9 collective-permute-start.13
  878.9 4.5 collective-permute-start.14
  883.4 10.8 %collective-permute-start.15 = (bf16[1,16,256]{2,1,0:T(8,128)(2,1)S(1)}, bf16[1,16,256]{2,1,0:T(8,128)(2,1)S(1)}, u32[]{:S(2)}, u32[]{:S(2)}) collective-permute-start(bf16[1,16,256]{2,1,0:T(8,128)(2,1)S(1)} %select_convert_fusion.16), channel_id=1, source_target_pairs={{0,16},{16,0},{32,48},{48,32},{64,80},{80,64},{96,112},{112,96},{1... | collective-permute-start | bytes 24584 | tf_op jit(solution)/shard_map/ppermute | solution.py:8
  894.3 88.3 %copy-start.11 = (bf16[16,256]{1,0:T(8,128)(2,1)}, bf16[16,256]{1,0:T(8,128)(2,1)S(1)}, u32[]{:S(2)}) copy-start(bf16[16,256]{1,0:T(8,128)(2,1)S(1)} %fusion.37) | copy-start | bytes 24580
  911.7 8.3 collective-permute-start.16
  936.2 68.1 %copy-start.6 = (bf16[1024,256]{1,0:T(8,128)(2,1)S(1)}, bf16[1024,256]{1,0:T(8,128)(2,1)}, u32[]{:S(2)}) copy-start(bf16[1024,256]{1,0:T(8,128)(2,1)} %copy-done.5) | copy-start | bytes 1572868
  936.2 68.1 %copy-start.10 = (bf16[32,1024]{1,0:T(8,128)(2,1)S(1)}, bf16[32,1024]{1,0:T(8,128)(2,1)}, u32[]{:S(2)}) copy-start(bf16[32,1024]{1,0:T(8,128)(2,1)} %param.14) | copy-start | bytes 196612
  936.2 6.3 collective-permute-start.17
  942.5 5.0 collective-permute-start.18
  947.5 17.2 %collective-permute-start.19 = (bf16[1,32,256]{2,1,0:T(8,128)(2,1)S(1)}, bf16[1,32,256]{2,1,0:T(8,128)(2,1)S(1)}, u32[]{:S(2)}, u32[]{:S(2)}) collective-permute-start(bf16[1,32,256]{2,1,0:T(8,128)(2,1)S(1)} %select_convert_fusion.11), channel_id=1, source_target_pairs={{0,16},{16,0},{32,48},{48,32},{64,80},{80,64},{96,112},{112,96},{1... | collective-permute-start | bytes 49160 | tf_op jit(solution)/shard_map/ppermute | solution.py:8
  982.6 6.1 collective-permute-start.20
  988.7 4.7 collective-permute-start.21
  993.4 10.9 %collective-permute-start.22 = (bf16[1,32,256]{2,1,0:T(8,128)(2,1)S(1)}, bf16[1,32,256]{2,1,0:T(8,128)(2,1)S(1)}, u32[]{:S(2)}, u32[]{:S(2)}) collective-permute-start(bf16[1,32,256]{2,1,0:T(8,128)(2,1)S(1)} %select_convert_fusion.10), channel_id=1, source_target_pairs={{0,16},{16,0},{32,48},{48,32},{64,80},{80,64},{96,112},{112,96},{1... | collective-permute-start | bytes 49160 | tf_op jit(solution)/shard_map/ppermute | solution.py:8
  1004.3 2.2 copy-start.14
Sparse Core Ops, SparseCore 0:
  52.4 81.2 reduce-scatter.9
  191.2 81.0 reduce-scatter.11
  308.3 80.6 reduce-scatter.13
  439.0 109.3 all-reduce.4
  584.6 105.5 all-reduce.6
where the time goes:
time: 1010 us
  waiting for transfers between devices  534 us (53%)
  blocking collectives  293 us (29%)
  starting transfers between devices  147 us (15%)
  between operations  15.4 us (2%)
    unnamed x7, waiting for transfers between devices  215 us
    all_gather x5, blocking collectives, group_gather(): gathered = lax.all_gather(block, 'leaf', axis=0, tiled=True)  175 us
    reduce_scatter x2, waiting for transfers between devices, forward_front(): lax.psum_scatter(lax.dot_general(local_inverse, columns, (((0,), (0,)), (...  162 us
    ppermute x23, starting transfers between devices, partner(): lax.ppermute(array, axis, [(i, i ^ 1 << distance) for i in range(lax.axis...  146 us
    reduce_scatter x1, waiting for transfers between devices, forward_update(): lax.psum_scatter(both_sums.astype(jnp.bfloat16), 'front', scatter_dimensi...  80.4 us
    ppermute x23, waiting for transfers between devices, partner(): lax.ppermute(array, axis, [(i, i ^ 1 << distance) for i in range(lax.axis...  76.8 us
    all_gather x3, blocking collectives, backward_front(): lax.all_gather(solved_block, 'front', axis=0, tiled=True)  51 us
    all_gather x2, blocking collectives, backward_update(): lax.all_gather(sibling_block, 'front', axis=0, tiled=True)  33.8 us
  transfers between devices with their start and end apart: 28, of which 28 were waited for; matrix products, arithmetic and copies ran while one was open for 0% of the time, Pallas kernels for 0%

commit v1 on v0

--- a/solution.py
+++ b/solution.py
@@ -1,7 +1,39 @@
+import functools
 import jax
 import jax.numpy as jnp
 from jax import lax
 from jax.sharding import PartitionSpec as P
+
+
+def pair_ways(content, which_axis):
+    outer, extra, mixed_arr = (
+        jax.lax.axis_size(which_axis),
+        jax.lax.axis_index(which_axis),
+        content.shape[0],
+    )
+    sheets = tuple((at * outer if c == 0 else at for c, at in enumerate(content.shape)))
+    w1 = lax.dynamic_update_slice_in_dim(
+        jnp.zeros(sheets, content.dtype), content, extra * mixed_arr, axis=0
+    )
+    tile_out = current_arr = content
+    t = 1
+    while t < outer // 2 + 1:
+        tile_out = jax.lax.ppermute(
+            tile_out, axis_name=which_axis, perm=tuple(((c, (c + 1) % outer) for c in range(outer)))
+        )
+        w1 = lax.dynamic_update_slice_in_dim(w1, tile_out, (extra - t) % outer * mixed_arr, axis=0)
+        if 2 * t < outer:
+            current_arr = jax.lax.ppermute(
+                current_arr, which_axis, tuple(((c, (c - 1) % outer) for c in range(outer)))
+            )
+            w1 = lax.dynamic_update_slice_in_dim(
+                w1, current_arr, (extra + t) % outer * mixed_arr, axis=0
+            )
+        t += 1
+    return w1
+
+
+drive_matrix = functools.partial(pair_ways, which_axis="front")
 
 
 def partner(array, axis, distance):
@@ -118,10 +150,7 @@
     initial = jnp.zeros((groups * pieces, parent_solution.shape[1]), jnp.float32)
     partial_value = add_rows(
         initial,
-        (
-            lax.all_gather(parent_solution, "front", axis=0, tiled=True),
-            lax.all_gather(sibling_block, "front", axis=0, tiled=True),
-        ),
+        (lax.all_gather(parent_solution, "front", axis=0, tiled=True), drive_matrix(sibling_block)),
         jnp.int32(0),
     )
     summed = group_reduce(partial_value, groups)

time: 1010 us -> 1120 us (1.11)
  starting transfers between devices: 147 us -> 271 us
  blocking collectives: 293 us -> 258 us
    ppermute x0 -> x30, starting transfers between devices: none -> 124 us  [the longest x14 92.7 us: pair_ways(): jax.lax.ppermute(current_arr, which_axis, tuple(((c, (c - 1) % outer) for...]
    all_gather x2 -> x0, blocking collectives: 33.8 us -> none  [backward_update(): lax.all_gather(sibling_block, 'front', axis=0, tiled=True)]
    ppermute x0 -> x30, waiting for transfers between devices: none -> 11.5 us  [the longest x16 11.5 us: pair_ways(): jax.lax.ppermute(tile_out, axis_name=which_axis, perm=tuple(((c, (c + 1)...]
  transfers between devices with their start and end apart: 28 -> 58, of which waited for: 28 -> 30; matrix products, arithmetic and copies ran while one was open for 0% -> 0% of each run, Pallas kernels for 0% -> 0%
where the time goes in v1:
time: 1120 us; the launch traced here: 1110 us
  waiting for transfers between devices  544 us (49%)
  starting transfers between devices  271 us (24%)
  blocking collectives  258 us (23%)
  between operations  16.6 us (1%)
    unnamed x7, waiting for transfers between devices  215 us
    all_gather x5, blocking collectives, group_gather(): gathered = lax.all_gather(block, 'leaf', axis=0, tiled=True)  175 us
    reduce_scatter x2, waiting for transfers between devices, forward_front(): lax.psum_scatter(lax.dot_general(local_inverse, columns, (((0,), (0,)), (...  162 us
    ppermute x23, starting transfers between devices, partner(): lax.ppermute(array, axis, [(i, i ^ 1 << distance) for i in range(lax.axis...  146 us
    ppermute x14, starting transfers between devices, pair_ways(): jax.lax.ppermute(current_arr, which_axis, tuple(((c, (c - 1) % outer) for...  92.7 us
    reduce_scatter x1, waiting for transfers between devices, forward_update(): lax.psum_scatter(both_sums.astype(jnp.bfloat16), 'front', scatter_dimensi...  80.4 us
    ppermute x23, waiting for transfers between devices, partner(): lax.ppermute(array, axis, [(i, i ^ 1 << distance) for i in range(lax.axis...  75.5 us
    all_gather x3, blocking collectives, backward_front(): lax.all_gather(solved_block, 'front', axis=0, tiled=True)  48.4 us
  transfers between devices with their start and end apart: 58, of which 30 were waited for; matrix products, arithmetic and copies ran while one was open for 0% of the time, Pallas kernels for 0%

profile of v1, /device:TPU:1, one launch (start us, length us, event | category | flops | bytes accessed | tf_op | source)
XLA Modules:
  0.0 1113.0 jit_solution(6875692309507413514)
XLA Ops:
  12.2 39.0 %all_gather.30 = bf16[1024,256]{1,0:T(8,128)(2,1)S(1)} all-gather(bf16[32,256]{1,0:T(8,128)(2,1)S(1)} %fusion.8), channel_id=1, replica_groups=mesh['leaf'=32,'front'=16] {'leaf'}, dimensions={0}, use_global_device_ids=true | all-gather | bytes 540672 | tf_op jit(solution)/shard_map/all_gather | solution.py:58
  52.5 81.3 %reduce-scatter.10.cloned.1.call-done = bf16[32,256]{1,0:T(8,128)(2,1)} async-done(((bf16[512,256]{1,0:T(8,128)(2,1)}), bf16[32,256]{1,0:T(8,128)(2,1)}) %reduce-scatter.10.cloned.1.call-update) | async-done | bytes 16400 | tf_op jit(solution)/shard_map/reduce_scatter | solution.py:84
  134.5 34.5 %all_gather.31 = bf16[1024,256]{1,0:T(8,128)(2,1)S(1)} all-gather(bf16[32,256]{1,0:T(8,128)(2,1)S(1)} %select_convert_fusion.15), channel_id=1, replica_groups=mesh['leaf'=32,'front'=16] {'leaf'}, dimensions={0}, use_global_device_ids=true | all-gather | bytes 540672 | tf_op jit(solution)/shard_map/all_gather | solution.py:58
  170.0 4.7 collective-permute-start
  174.9 14.5 %collective-permute-done = bf16[256,256]{0,1:T(8,128)(2,1)} collective-permute-done((bf16[256,256]{0,1:T(8,128)(2,1)S(1)}, bf16[256,256]{0,1:T(8,128)(2,1)}, u32[]{:S(2)}, u32[]{:S(2)}) %collective-permute-start) | collective-permute-done | bytes 131104 | tf_op jit(solution)/shard_map/ppermute | solution.py:40
  191.8 80.4 %reduce-scatter.12.cloned.1.call-done = bf16[16,256]{1,0:T(8,128)(2,1)} async-done(((bf16[256,256]{1,0:T(8,128)(2,1)}), bf16[16,256]{1,0:T(8,128)(2,1)}) %reduce-scatter.12.cloned.1.call-update) | async-done | bytes 8208 | tf_op jit(solution)/shard_map/reduce_scatter | solution.py:112
  273.0 34.1 %all_gather.32 = bf16[512,256]{1,0:T(8,128)(2,1)S(1)} all-gather(bf16[16,256]{1,0:T(8,128)(2,1)S(1)} %select_convert_fusion.20), channel_id=1, replica_groups=mesh['leaf'=32,'front'=16] {'leaf'}, dimensions={0}, use_global_device_ids=true | all-gather | bytes 270336 | tf_op jit(solution)/shard_map/all_gather | solution.py:58
  308.2 80.6 %reduce-scatter.14.cloned.1.call-done = bf16[16,256]{1,0:T(8,128)(2,1)} async-done(((bf16[256,256]{1,0:T(8,128)(2,1)}), bf16[16,256]{1,0:T(8,128)(2,1)}) %reduce-scatter.14.cloned.1.call-update) | async-done | bytes 8208 | tf_op jit(solution)/shard_map/reduce_scatter | solution.py:84
  389.6 34.1 %all_gather.33 = bf16[512,256]{1,0:T(8,128)(2,1)S(1)} all-gather(bf16[16,256]{1,0:T(8,128)(2,1)S(1)} %select_convert_fusion.19), channel_id=1, replica_groups=mesh['leaf'=32,'front'=16] {'leaf'}, dimensions={0}, use_global_device_ids=true | all-gather | bytes 270336 | tf_op jit(solution)/shard_map/all_gather | solution.py:58
  424.0 8.9 collective-permute-start.1
  439.5 108.8 %all-reduce.5.cloned.1.call-done = bf16[128,256]{1,0:T(8,128)(2,1)} async-done(((bf16[128,256]{1,0:T(8,128)(2,1)}), bf16[128,256]{1,0:T(8,128)(2,1)}) %all-reduce.5.cloned.1.call-update) | async-done | bytes 65552
  549.1 33.4 %all_gather.34 = bf16[256,256]{1,0:T(8,128)(2,1)S(1)} all-gather(bf16[8,256]{1,0:T(8,128)(2,1)S(1)} %select_convert_fusion.23), channel_id=1, replica_groups=mesh['leaf'=32,'front'=16] {'leaf'}, dimensions={0}, use_global_device_ids=true | all-gather | bytes 135168 | tf_op jit(solution)/shard_map/all_gather | solution.py:58
  584.3 105.7 %all-reduce.7.cloned.1.call-done = bf16[128,256]{1,0:T(8,128)(2,1)} async-done(((bf16[128,256]{1,0:T(8,128)(2,1)}), bf16[128,256]{1,0:T(8,128)(2,1)}) %all-reduce.7.cloned.1.call-update) | async-done | bytes 65552
  690.7 17.5 %all_gather.35 = bf16[128,256]{1,0:T(8,128)(2,1)S(1)} all-gather(bf16[8,256]{1,0:T(8,128)(2,1)S(1)} %select_convert_fusion.22), channel_id=1, replica_groups=mesh['leaf'=32,'front'=16] {'front'}, dimensions={0}, use_global_device_ids=true | all-gather | bytes 69632 | tf_op jit(solution)/shard_map/all_gather | solution.py:128
  709.2 12.5 %collective-permute-start.2 = (bf16[16,8,256]{2,1,0:T(8,128)(2,1)S(1)}, bf16[16,8,256]{2,1,0:T(8,128)(2,1)S(1)}, u32[]{:S(2)}, u32[]{:S(2)}) collective-permute-start(bf16[16,8,256]{2,1,0:T(8,128)(2,1)S(1)} %fusion.26), channel_id=1, source_target_pairs={{0,256},{16,272},{32,288},{48,304},{64,320},{80,336},{96,352},{112... | collective-permute-start | bytes 196616 | tf_op jit(solution)/shard_map/ppermute | solution.py:40
  723.7 7.9 collective-permute-start.3
  745.4 12.3 %collective-permute-start.6 = (bf16[1,8,256]{2,1,0:T(8,128)(2,1)S(1)}, bf16[1,8,256]{2,1,0:T(8,128)(2,1)S(1)}, u32[]{:S(2)}, u32[]{:S(2)}) collective-permute-start(bf16[1,8,256]{2,1,0:T(8,128)(2,1)S(1)} %select_convert_fusion.21), channel_id=1, source_target_pairs={{0,16},{16,0},{32,48},{48,32},{64,80},{80,64},{96,112},{112,96},{1... | collective-permute-start | bytes 12296 | tf_op jit(solution)/shard_map/ppermute | solution.py:40
  758.6 15.9 %all_gather.36 = bf16[128,256]{1,0:T(8,128)(2,1)S(1)} all-gather(bf16[8,256]{1,0:T(8,128)(2,1)S(1)} %fusion.48), channel_id=1, replica_groups=mesh['leaf'=32,'front'=16] {'front'}, dimensions={0}, use_global_device_ids=true | all-gather | bytes 69632 | tf_op jit(solution)/shard_map/all_gather | solution.py:153
  774.5 13.3 %collective-permute-start.7 = (bf16[8,256]{1,0:T(8,128)(2,1)S(1)}, bf16[8,256]{1,0:T(8,128)(2,1)S(1)}, u32[]{:S(2)}, u32[]{:S(2)}) collective-permute-start(bf16[8,256]{1,0:T(8,128)(2,1)S(1)} %fusion.48), channel_id=1, source_target_pairs={{0,256},{16,272},{32,288},{48,304},{64,320},{80,336},{96,352},{112... | collective-permute-start | bytes 12296 | tf_op jit(solution)/shard_map/ppermute | solution.py:40
  791.7 5.8 collective-permute-start.9
  799.5 6.7 collective-permute-start.11
  808.1 6.7 collective-permute-start.13
  816.8 6.7 collective-permute-start.15
  825.5 6.7 collective-permute-start.17
  834.2 6.7 collective-permute-start.19
  842.8 6.7 collective-permute-start.21
  851.5 5.7 collective-permute-done.22
  857.4 5.6 collective-permute-start.23
  863.0 4.9 collective-permute-done.23
  878.3 16.8 %collective-permute-start.26 = (bf16[1,16,256]{2,1,0:T(8,128)(2,1)S(1)}, bf16[1,16,256]{2,1,0:T(8,128)(2,1)S(1)}, u32[]{:S(2)}, u32[]{:S(2)}) collective-permute-start(bf16[1,16,256]{2,1,0:T(8,128)(2,1)S(1)} %select_convert_fusion.17), channel_id=1, source_target_pairs={{0,16},{16,0},{32,48},{48,32},{64,80},{80,64},{96,112},{112,96},{1... | collective-permute-start | bytes 24584 | tf_op jit(solution)/shard_map/ppermute | solution.py:40
  896.1 15.4 %all_gather.37 = bf16[256,256]{1,0:T(8,128)(2,1)S(1)} all-gather(bf16[16,256]{1,0:T(8,128)(2,1)S(1)} %fusion.39), channel_id=1, replica_groups=mesh['leaf'=32,'front'=16] {'front'}, dimensions={0}, use_global_device_ids=true | all-gather | bytes 139264 | tf_op jit(solution)/shard_map/all_gather | solution.py:128
  911.7 4.6 collective-permute-start.27
  916.2 5.5 collective-permute-done.27
  923.7 4.6 collective-permute-done.28
  932.8 10.0 collective-permute-start.30
  943.7 18.3 %all_gather.38 = bf16[256,256]{1,0:T(8,128)(2,1)S(1)} all-gather(bf16[16,256]{1,0:T(8,128)(2,1)S(1)} %fusion.37), channel_id=1, replica_groups=mesh['leaf'=32,'front'=16] {'front'}, dimensions={0}, use_global_device_ids=true | all-gather | bytes 139264 | tf_op jit(solution)/shard_map/all_gather | solution.py:153
  965.9 4.4 collective-permute-done.31
  972.2 6.7 collective-permute-start.33
  980.9 6.7 collective-permute-start.35
  989.6 6.7 collective-permute-start.37
  998.2 6.7 collective-permute-start.39
  1006.9 6.7 collective-permute-start.41
  1015.6 6.7 collective-permute-start.43
  1024.3 6.7 collective-permute-start.45
  1033.0 5.7 collective-permute-done.46
  1050.3 16.0 %collective-permute-start.49 = (bf16[1,32,256]{2,1,0:T(8,128)(2,1)S(1)}, bf16[1,32,256]{2,1,0:T(8,128)(2,1)S(1)}, u32[]{:S(2)}, u32[]{:S(2)}) collective-permute-start(bf16[1,32,256]{2,1,0:T(8,128)(2,1)S(1)} %select_convert_fusion.11), channel_id=1, source_target_pairs={{0,16},{16,0},{32,48},{48,32},{64,80},{80,64},{96,112},{112,96},{1... | collective-permute-start | bytes 49160 | tf_op jit(solution)/shard_map/ppermute | solution.py:40
  1067.1 15.5 %all_gather.39 = bf16[512,256]{1,0:T(8,128)(2,1)S(1)} all-gather(bf16[32,256]{1,0:T(8,128)(2,1)S(1)} %fusion.36), channel_id=1, replica_groups=mesh['leaf'=32,'front'=16] {'front'}, dimensions={0}, use_global_device_ids=true | all-gather | bytes 278528 | tf_op jit(solution)/shard_map/all_gather | solution.py:128
  1093.7 9.7 collective-permute-start.52
  (237 shorter events, 121.6 us)
Async XLA Ops:
  7.2 126.5 %reduce-scatter.10.cloned.1.call-start = ((), (), s32[]{:S(2)}) async-start(), calls=%async_computation.3 | async-start | bytes 278528 | tf_op jit(solution)/shard_map/reduce_scatter | solution.py:84
  52.3 219.9 %reduce-scatter.12.cloned.1.call-start = ((), (), s32[]{:S(2)}) async-start(), calls=%async_computation.4 | async-start | bytes 139264 | tf_op jit(solution)/shard_map/reduce_scatter | solution.py:112
  170.0 19.4 %collective-permute-start = (bf16[256,256]{0,1:T(8,128)(2,1)S(1)}, bf16[256,256]{0,1:T(8,128)(2,1)}, u32[]{:S(2)}, u32[]{:S(2)}) collective-permute-start(bf16[256,256]{0,1:T(8,128)(2,1)S(1)} %bitcast.156), channel_id=1, source_target_pairs={{0,128},{16,144},{32,160},{48,176},{64,192},{80,208},{96,224},{112... | collective-permute-start | bytes 393224 | tf_op jit(solution)/shard_map/ppermute | solution.py:40
  191.1 197.7 %reduce-scatter.14.cloned.1.call-start = ((), (), s32[]{:S(2)}) async-start(), calls=%async_computation.5 | async-start | bytes 139264 | tf_op jit(solution)/shard_map/reduce_scatter | solution.py:84
  308.1 240.2 %all-reduce.5.cloned.1.call-start = ((), (), s32[]{:S(2)}) async-start(), calls=%async_computation.6 | async-start | bytes 131072
  424.0 14.2 %collective-permute-start.1 = (bf16[128,256]{1,0:T(8,128)(2,1)S(1)}, bf16[128,256]{1,0:T(8,128)(2,1)S(1)}, u32[]{:S(2)}, u32[]{:S(2)}) collective-permute-start(bf16[128,256]{1,0:T(8,128)(2,1)S(1)} %fusion.25), channel_id=1, source_target_pairs={{0,256},{16,272},{32,288},{48,304},{64,320},{80,336},{96,352},{112... | collective-permute-start | bytes 196616 | tf_op jit(solution)/shard_map/ppermute | solution.py:40
  438.8 251.2 %all-reduce.7.cloned.1.call-start = ((), (), s32[]{:S(2)}) async-start(), calls=%async_computation.7 | async-start | bytes 131072
  709.2 14.5 %collective-permute-start.2 = (bf16[16,8,256]{2,1,0:T(8,128)(2,1)S(1)}, bf16[16,8,256]{2,1,0:T(8,128)(2,1)S(1)}, u32[]{:S(2)}, u32[]{:S(2)}) collective-permute-start(bf16[16,8,256]{2,1,0:T(8,128)(2,1)S(1)} %fusion.26), channel_id=1, source_target_pairs={{0,256},{16,272},{32,288},{48,304},{64,320},{80,336},{96,352},{112... | collective-permute-start | bytes 196616 | tf_op jit(solution)/shard_map/ppermute | solution.py:40
  723.7 11.9 %collective-permute-start.3 = (bf16[8,8,256]{2,1,0:T(8,128)(2,1)S(1)}, bf16[8,8,256]{2,1,0:T(8,128)(2,1)S(1)}, u32[]{:S(2)}, u32[]{:S(2)}) collective-permute-start(bf16[8,8,256]{2,1,0:T(8,128)(2,1)S(1)} %select_convert_fusion.9), channel_id=1, source_target_pairs={{0,128},{16,144},{32,160},{48,176},{64,192},{80,208},{96,224},{112... | collective-permute-start | bytes 98312 | tf_op jit(solution)/shard_map/ppermute | solution.py:40
  745.4 13.1 %collective-permute-start.6 = (bf16[1,8,256]{2,1,0:T(8,128)(2,1)S(1)}, bf16[1,8,256]{2,1,0:T(8,128)(2,1)S(1)}, u32[]{:S(2)}, u32[]{:S(2)}) collective-permute-start(bf16[1,8,256]{2,1,0:T(8,128)(2,1)S(1)} %select_convert_fusion.21), channel_id=1, source_target_pairs={{0,16},{16,0},{32,48},{48,32},{64,80},{80,64},{96,112},{112,96},{1... | collective-permute-start | bytes 12296 | tf_op jit(solution)/shard_map/ppermute | solution.py:40
  774.5 14.3 %collective-permute-start.7 = (bf16[8,256]{1,0:T(8,128)(2,1)S(1)}, bf16[8,256]{1,0:T(8,128)(2,1)S(1)}, u32[]{:S(2)}, u32[]{:S(2)}) collective-permute-start(bf16[8,256]{1,0:T(8,128)(2,1)S(1)} %fusion.48), channel_id=1, source_target_pairs={{0,256},{16,272},{32,288},{48,304},{64,320},{80,336},{96,352},{112... | collective-permute-start | bytes 12296 | tf_op jit(solution)/shard_map/ppermute | solution.py:40
  788.9 8.6 collective-permute-start.8
  791.7 7.8 collective-permute-start.9
  797.5 8.7 collective-permute-start.10
  799.5 8.7 collective-permute-start.11
  806.2 8.7 collective-permute-start.12
  808.1 8.7 collective-permute-start.13
  814.9 8.7 collective-permute-start.14
  816.8 8.7 collective-permute-start.15
  823.5 8.7 collective-permute-start.16
  825.5 8.7 collective-permute-start.17
  832.2 8.7 collective-permute-start.18
  834.2 8.7 collective-permute-start.19
  840.9 8.7 collective-permute-start.20
  842.8 8.7 collective-permute-start.21
  849.6 7.7 collective-permute-start.22
  857.4 10.5 collective-permute-start.23
  878.3 17.6 %collective-permute-start.26 = (bf16[1,16,256]{2,1,0:T(8,128)(2,1)S(1)}, bf16[1,16,256]{2,1,0:T(8,128)(2,1)S(1)}, u32[]{:S(2)}, u32[]{:S(2)}) collective-permute-start(bf16[1,16,256]{2,1,0:T(8,128)(2,1)S(1)} %select_convert_fusion.17), channel_id=1, source_target_pairs={{0,16},{16,0},{32,48},{48,32},{64,80},{80,64},{96,112},{112,96},{1... | collective-permute-start | bytes 24584 | tf_op jit(solution)/shard_map/ppermute | solution.py:40
  911.7 10.1 collective-permute-start.27
  932.8 10.8 collective-permute-start.30
  962.0 8.3 collective-permute-start.31
  970.3 8.6 collective-permute-start.32
  972.2 8.7 collective-permute-start.33
  979.0 8.7 collective-permute-start.34
  980.9 8.7 collective-permute-start.35
  987.6 8.7 collective-permute-start.36
  989.6 8.7 collective-permute-start.37
  996.3 8.7 collective-permute-start.38
  998.2 8.7 collective-permute-start.39
  1005.0 8.7 collective-permute-start.40
  1006.9 8.7 collective-permute-start.41
  1013.7 8.7 collective-permute-start.42
  1015.6 8.7 collective-permute-start.43
  1022.3 8.7 collective-permute-start.44
  1024.3 8.7 collective-permute-start.45
  1031.0 7.7 collective-permute-start.46
  1050.3 16.8 %collective-permute-start.49 = (bf16[1,32,256]{2,1,0:T(8,128)(2,1)S(1)}, bf16[1,32,256]{2,1,0:T(8,128)(2,1)S(1)}, u32[]{:S(2)}, u32[]{:S(2)}) collective-permute-start(bf16[1,32,256]{2,1,0:T(8,128)(2,1)S(1)} %select_convert_fusion.11), channel_id=1, source_target_pairs={{0,16},{16,0},{32,48},{48,32},{64,80},{80,64},{96,112},{112,96},{1... | collective-permute-start | bytes 49160 | tf_op jit(solution)/shard_map/ppermute | solution.py:40
  1093.7 10.5 collective-permute-start.52
  (29 other events, 1860.5 us)
Sparse Core Ops, SparseCore 0:
  52.5 81.2 reduce-scatter.9
  191.2 80.9 reduce-scatter.11
  308.2 80.5 reduce-scatter.13
  438.9 109.3 all-reduce.4
  584.4 105.5 all-reduce.6
